TPU v7x, 32 devices: a whole 2x2x4 slice. The times are simulated.
32 devices in a mesh: dp: 4 (over z), section: 2 (over core), tensor: 4 (over y, x).
Axes of the slice: x: 2, y: 2, z: 4, core: 2. Of those that a mesh axis runs over, the one named last changes fastest.
Arguments:
- tokens: bfloat16 [1024, 8192], P('dp', 'tensor'), may hold values from -6 to 6
- dest_slot: int32 [1024], P('dp'), may hold values from 0 to 1023, as said below
- doc_reset: int32 [1024], P('dp'), may hold values 0 or 1
- norm_gain: float32 [2, 8192], P('section'), may hold values from 0.25 to 1.75
- w_in: bfloat16 [2, 8192, 5120], P('section', 'dp', 'tensor'), may hold values from -0.0625 to 0.0625
- w_step: bfloat16 [2, 8192, 32], P('section', None, 'tensor'), may hold values from -0.0625 to 0.0625
- step_bias: float32 [2, 32], P('section', 'tensor'), may hold values from -4 to -1.5
- a_log: float32 [2, 32], P('section', 'tensor'), may hold values from -2.5 to 1.5
- d_skip: float32 [2, 32], P('section', 'tensor'), may hold values from 0.3 to 2
- out_gain: float32 [2, 2048], P('section', 'tensor'), may hold values from 0.25 to 1.75
- w_out: bfloat16 [2, 2048, 8192], P('section', 'tensor'), may hold values from -0.125 to 0.125
Outputs:
- phase_out: bfloat16 [2, 1024, 8192], P('section', 'dp', 'tensor')
Inputs may be any that keep to these rules, and one draw needn't show every extreme that they name: dest_slot is a permutation; the tokens of one group go in order to increasing groups, and each group receives rows in order of source group. One group sends at most 128 tokens to one group, and every group sends exactly 128 to some group.
All inputs are finite; a program needn't handle non-finite values. No bound on the sum of `doc_reset` on one device may be relied on, other than what follows from the above.
Results may differ from a plain program's by a relative error of at most 0.018.
Values may be sent and summed in bfloat16 or wider, within the bound.
A program may use at most 128 MiB of HBM per device.

v0:
```python
import jax
import jax.numpy as jnp
from jax import lax
from jax.sharding import PartitionSpec as P

HEAD_DIM = 64
STATE = 128
HEADS_DEV = 8
SPAN = 64
epsilon = 1e-05


def scan_block(inputs, writes, readout, step_size, log_decay, resets, state, skips):
    segment = jnp.cumsum(resets)
    cumulative = jnp.cumsum(log_decay, axis=0)
    positions = jnp.arange(resets.shape[0])
    in_segment = (segment[:, None] == segment[None, :]) & (positions[:, None] >= positions[None, :])
    by_head = cumulative.T
    gap = by_head[:, :, None] - by_head[:, None, :]
    decayed = jnp.where(in_segment[None], jnp.exp(jnp.where(in_segment[None], gap, 0.0)), 0.0)
    f32 = jnp.float32
    scores = jnp.einsum("tn,sn->ts", readout, writes, preferred_element_type=f32)
    weights = scores[None] * decayed * step_size.T[:, None, :]
    output = jnp.einsum("hts,shp->thp", weights, inputs.astype(f32))
    carry_ok = (segment == 0).astype(f32)
    carried = jnp.einsum("tn,hpn->thp", readout.astype(f32), state)
    output = output + carry_ok[:, None, None] * jnp.exp(cumulative)[:, :, None] * carried
    last_seg = segment[-1]
    tail = (
        (segment == last_seg).astype(f32)[:, None]
        * jnp.exp(cumulative[-1][None, :] - cumulative)
        * step_size
    )
    fresh = jnp.einsum("shp,sn->hpn", tail[:, :, None] * inputs.astype(f32), writes.astype(f32))
    kept = (last_seg == 0).astype(f32) * jnp.exp(cumulative[-1])[:, None, None] * state
    output = output + skips[None, :, None] * inputs.astype(f32)
    return (output, fresh + kept)


def per_device(
    tokens, dest_slot, doc_reset, norm_gain, w_in, w_step, step_bias, a_log, d_skip, out_gain, w_out
):
    f32, bf16 = (jnp.float32, jnp.bfloat16)
    groups = lax.axis_size("dp")
    width = lax.axis_size("tensor")
    cores = lax.axis_size("section")
    layers = cores
    dp_idx = lax.axis_index("dp")
    core = lax.axis_index("section")
    row_count = tokens.shape[0]
    feat_local = tokens.shape[1]
    feats = feat_local * width
    capacity = 2 * row_count // groups
    head_cols = HEADS_DEV * HEAD_DIM

    def whole(param):
        return lax.all_gather(param, "section", axis=0, tiled=True)

    w_in, w_out, w_step = (whole(w_in), whole(w_out), whole(w_step))
    norm_gain, step_bias, a_log, d_skip, out_gain = (
        whole(norm_gain),
        whole(step_bias),
        whole(a_log),
        whole(d_skip),
        whole(out_gain),
    )
    part = feat_local // cores
    mine = lax.dynamic_slice_in_dim(tokens, core * part, part, axis=1)
    target = dest_slot // row_count
    onehot = (target[:, None] == jnp.arange(groups)[None, :]).astype(jnp.int32)
    before = jnp.cumsum(onehot, axis=0) - onehot
    placed = jnp.sum(onehot * before, axis=1)
    slots = target * capacity + placed
    outbox = jnp.zeros((groups * capacity, part), bf16).at[slots].set(mine)
    marks = (
        jnp.full((groups * capacity,), row_count, jnp.int32).at[slots].set(dest_slot % row_count)
    )
    inbox = lax.all_to_all(
        outbox.reshape(groups, capacity, part), "dp", split_axis=0, concat_axis=0, tiled=True
    )
    where_to = lax.all_to_all(
        marks.reshape(groups, capacity), "dp", split_axis=0, concat_axis=0, tiled=True
    )
    balanced = (
        jnp.zeros((row_count, part), bf16)
        .at[where_to.reshape(-1)]
        .set(inbox.reshape(-1, part), mode="drop")
    )
    few = row_count // (cores * width)
    half = row_count // cores
    rows = lax.all_to_all(
        balanced.reshape(cores * width, few, part), ("section", "tensor"), 0, 0, tiled=True
    )
    rows = rows.reshape(cores, width, few, part).transpose(2, 1, 0, 3).reshape(few, feats)
    depth = w_in.shape[1]
    outs = []
    for layer in range(layers):
        widened = rows.astype(f32)
        meansq = jnp.mean(widened * widened, axis=-1, keepdims=True)
        u = (widened * lax.rsqrt(meansq + epsilon) * norm_gain[layer]).astype(bf16)
        u = u.reshape(few, groups, depth).transpose(1, 0, 2)
        u = lax.all_to_all(u, "dp", 0, 0, tiled=True)
        step_w = lax.dynamic_slice_in_dim(w_step[layer], dp_idx * depth, depth, axis=0)
        full_u = lax.all_gather(u, "tensor", axis=1, tiled=True)
        full_u = full_u.reshape(groups * half, depth)
        proj = jnp.dot(full_u, w_in[layer], preferred_element_type=f32).astype(bf16)
        pre = jnp.dot(full_u, step_w, preferred_element_type=f32)
        proj = lax.all_to_all(proj.reshape(groups, half, -1), "dp", 0, 0, tiled=True)
        pre = lax.all_to_all(pre.reshape(groups, half, HEADS_DEV), "dp", 0, 0, tiled=True)
        proj = jnp.sum(proj.astype(f32), axis=0).astype(bf16)
        pre = jnp.sum(pre, axis=0)
        proj = lax.all_gather(proj, "section", axis=0, tiled=True)
        pre = lax.all_gather(pre, "section", axis=0, tiled=True)
        step_size = jax.nn.softplus(pre + step_bias[layer])
        log_decay = -jnp.exp(a_log[layer]) * step_size
        state = jnp.zeros((HEADS_DEV, HEAD_DIM, STATE), f32)
        mixed = []
        for at in range(0, row_count, SPAN):
            span = slice(at, at + SPAN)
            output, state = scan_block(
                proj[span, head_cols : 2 * head_cols].reshape(SPAN, HEADS_DEV, HEAD_DIM),
                proj[span, 2 * head_cols : 2 * head_cols + STATE],
                proj[span, 2 * head_cols + STATE :],
                step_size[span],
                log_decay[span],
                doc_reset[span],
                state,
                d_skip[layer],
            )
            mixed.append(output.reshape(SPAN, head_cols))
        mixed = jnp.concatenate(mixed, axis=0)
        mixed = lax.dynamic_slice_in_dim(mixed, core * half, half, axis=0)
        gate = lax.dynamic_slice_in_dim(proj[:, :head_cols], core * half, half, axis=0).astype(f32)
        gated = mixed * jax.nn.silu(gate)
        meansq_out = jnp.mean(gated * gated, axis=-1, keepdims=True)
        normed = (gated * lax.rsqrt(meansq_out + epsilon) * out_gain[layer]).astype(bf16)
        partial_value = jnp.dot(normed, w_out[layer], preferred_element_type=f32).astype(bf16)
        partial_value = lax.all_to_all(
            partial_value.reshape(width, few, feats), "tensor", 0, 0, tiled=True
        )
        summed = jnp.sum(partial_value.astype(f32), axis=0)
        rows = (widened + summed).astype(bf16)
        outs.append(rows.reshape(few, width, feat_local).transpose(1, 0, 2))
    outs = jnp.concatenate(outs, axis=0)
    outs = lax.all_to_all(outs, ("section", "tensor"), 0, 0, tiled=True)
    return outs.reshape(1, row_count, feat_local)


def solution(mesh):
    placed = (
        P("dp", "tensor"),
        P("dp"),
        P("dp"),
        P("section", None),
        P("section", "dp", "tensor"),
        P("section", None, "tensor"),
        P("section", "tensor"),
        P("section", "tensor"),
        P("section", "tensor"),
        P("section", "tensor"),
        P("section", "tensor", None),
    )
    return jax.shard_map(
        per_device,
        mesh=mesh,
        in_specs=placed,
        out_specs=P("section", "dp", "tensor"),
        check_vma=False,
    )
```

profile of v0, /device:TPU:0, one launch (start us, length us, event | category | flops | bytes accessed | tf_op | source)
XLA Modules:
  0.0 413.6 jit_solution(3138068230953162979)
XLA Ops:
  10.9 6.3 %all-to-all-start = ((s32[4,1,128]{2,1,0:T(1,128)}), s32[4,1,128]{2,1,0:T(1,128)S(1)}, u32[]{:S(2)}, u32[]{:S(2)}) async-start(s32[4,1,128]{2,1,0:T(1,128)} %bitcast.3), calls=%async_computation | async-start | bytes 4096 | tf_op jit(solution)/shard_map/all_to_all | solution.py:81
  26.3 24.7 %all-to-all-done.1 = bf16[4,128,1024]{2,1,0:T(8,128)(2,1)S(1)} async-done(((bf16[4,128,1024]{2,1,0:T(8,128)(2,1)}), bf16[4,128,1024]{2,1,0:T(8,128)(2,1)S(1)}, u32[]{:S(2)}, u32[]{:S(2)}) %all-to-all-start.1) | async-done | bytes 1048608 | tf_op jit(solution)/shard_map/all_to_all | solution.py:78
  54.4 3.7 all-to-all-start.2
  60.8 6.4 %all-to-all-done.2 = bf16[8,32,1024]{2,1,0:T(8,128)(2,1)S(1)} async-done(((bf16[8,32,1024]{2,1,0:T(8,128)(2,1)}), bf16[8,32,1024]{2,1,0:T(8,128)(2,1)S(1)}, u32[]{:S(2)}, u32[]{:S(2)}) %all-to-all-start.2) | async-done | bytes 524320 | tf_op jit(solution)/shard_map/all_to_all | solution.py:91
  67.9 18.4 %all_to_all.64 = bf16[4,32,2048]{2,1,0:T(8,128)(2,1)} all-to-all(bf16[4,32,2048]{2,1,0:T(8,128)(2,1)S(1)} %fusion.28), channel_id=1, replica_groups=mesh['dp'=4,'section'=2,'tensor'=4] {'dp'}, dimensions={0} | all-to-all | bytes 1048576 | tf_op jit(solution)/shard_map/all_to_all | solution.py:102
  107.1 12.1 %all-gather.10.cloned.1.call-done = bf16[4,128,2048]{2,1,0:T(8,128)(2,1)} async-done(((bf16[4,32,2048]{2,1,0:T(8,128)(2,1)}), bf16[4,128,2048]{2,1,0:T(8,128)(2,1)}) %all-gather.10.cloned.1.call-update) | async-done | bytes 2097168 | tf_op jit(solution)/shard_map/all_gather | solution.py:104
  122.0 4.6 %all-to-all-start.5 = ((f32[4,128,8]{1,2,0:T(8,128)}), f32[4,128,8]{1,2,0:T(8,128)S(1)}, u32[]{:S(2)}, u32[]{:S(2)}) async-start(f32[4,128,8]{1,2,0:T(8,128)} %fusion.166), calls=%async_computation.5 | async-start | bytes 32768 | tf_op jit(solution)/shard_map/all_to_all | solution.py:109
  128.5 3.8 all-to-all-done.5
  136.1 7.3 %all-gather.12.cloned.1.call-done = bf16[2,2048,1280]{2,1,0:T(8,128)(2,1)} async-done(((bf16[1,2048,1280]{2,1,0:T(8,128)(2,1)}), bf16[2,2048,1280]{2,1,0:T(8,128)(2,1)}) %all-gather.12.cloned.1.call-update) | async-done | bytes 10485776 | tf_op jit(solution)/shard_map/all_gather | solution.py:57
  143.4 7.1 %fusion.2 = bf16[512,1280]{1,0:T(8,128)(2,1)} fusion(bf16[512,2048]{1,0:T(8,128)(2,1)} %bitcast.275, bf16[2,2048,1280]{2,1,0:T(8,128)(2,1)} %all-gather.12.cloned.1.call-done), kind=kOutput, calls=%fused_computation.13 | convolution fusion | flops 2685009920 | bytes 8650752 | tf_op jit(solution)/shard_map/dot_general | solution.py:106
  150.5 4.9 %all-to-all-start.4 = ((bf16[4,128,1280]{2,1,0:T(8,128)(2,1)}), bf16[4,128,1280]{2,1,0:T(8,128)(2,1)}, u32[]{:S(2)}, u32[]{:S(2)}) async-start(bf16[4,128,1280]{2,1,0:T(8,128)(2,1)} %bitcast.280), calls=%async_computation.4 | async-start | bytes 2621440 | tf_op jit(solution)/shard_map/all_to_all | solution.py:108
  159.4 27.9 %all-to-all-done.4 = bf16[4,128,1280]{2,1,0:T(8,128)(2,1)} async-done(((bf16[4,128,1280]{2,1,0:T(8,128)(2,1)}), bf16[4,128,1280]{2,1,0:T(8,128)(2,1)}, u32[]{:S(2)}, u32[]{:S(2)}) %all-to-all-start.4) | async-done | bytes 1310752 | tf_op jit(solution)/shard_map/all_to_all | solution.py:108
  205.0 6.0 %convolution_convert_fusion.1 = bf16[128,8192]{1,0:T(8,128)(2,1)} fusion(bf16[2,512,8192]{2,1,0:T(8,128)(2,1)} %all-gather.14.cloned.1.call-done, f32[128,512]{1,0:T(8,128)S(1)} %get-tuple-element.14, f32[512]{0:T(512)S(1)} %bitcast.326, f32[128]{0:T(128)S(1)} %add_rsqrt_fusion.2), kind=kOutput, calls=%fused_computation.4 | convolution fusion | flops 1074987008 | bytes 10750464 | tf_op jit(solution)/shard_map/dot_general | solution.py:137
  211.0 4.6 %all-to-all-start.6 = ((bf16[4,32,8192]{2,1,0:T(8,128)(2,1)}), bf16[4,32,8192]{2,1,0:T(8,128)(2,1)}, u32[]{:S(2)}, u32[]{:S(2)}) async-start(bf16[4,32,8192]{2,1,0:T(8,128)(2,1)} %bitcast.277), calls=%async_computation.6 | async-start | bytes 4194304 | tf_op jit(solution)/shard_map/all_to_all | solution.py:138
  215.8 25.4 %all-to-all-done.6 = bf16[4,32,8192]{2,1,0:T(8,128)(2,1)} async-done(((bf16[4,32,8192]{2,1,0:T(8,128)(2,1)}), bf16[4,32,8192]{2,1,0:T(8,128)(2,1)}, u32[]{:S(2)}, u32[]{:S(2)}) %all-to-all-start.6) | async-done | bytes 2097184 | tf_op jit(solution)/shard_map/all_to_all | solution.py:138
  247.2 17.3 %all_to_all.65 = bf16[4,32,2048]{2,1,0:T(8,128)(2,1)} all-to-all(bf16[4,32,2048]{2,1,0:T(8,128)(2,1)S(1)} %get-tuple-element.11), channel_id=1, replica_groups=mesh['dp'=4,'section'=2,'tensor'=4] {'dp'}, dimensions={0} | all-to-all | bytes 1048576 | tf_op jit(solution)/shard_map/all_to_all | solution.py:102
  264.6 33.5 %all-gather.16.cloned.1.call-done = bf16[4,128,2048]{2,1,0:T(8,128)(2,1)} async-done(((bf16[4,32,2048]{2,1,0:T(8,128)(2,1)}), bf16[4,128,2048]{2,1,0:T(8,128)(2,1)}) %all-gather.16.cloned.1.call-update) | async-done | bytes 2097168 | tf_op jit(solution)/shard_map/all_gather | solution.py:104
  301.0 4.6 %all-to-all-start.9 = ((f32[4,128,8]{1,2,0:T(8,128)}), f32[4,128,8]{1,2,0:T(8,128)S(1)}, u32[]{:S(2)}, u32[]{:S(2)}) async-start(f32[4,128,8]{1,2,0:T(8,128)} %fusion.164), calls=%async_computation.9 | async-start | bytes 32768 | tf_op jit(solution)/shard_map/all_to_all | solution.py:109
  305.6 6.4 %fusion.3 = bf16[512,1280]{1,0:T(8,128)(2,1)} fusion(bf16[512,2048]{1,0:T(8,128)(2,1)S(1)} %bitcast.276, bf16[2,2048,1280]{2,1,0:T(8,128)(2,1)} %all-gather.12.cloned.1.call-done), kind=kOutput, calls=%fused_computation.14 | convolution fusion | flops 2685009920 | bytes 8650752 | tf_op jit(solution)/shard_map/dot_general | solution.py:106
  312.1 5.1 %all-to-all-start.8 = ((bf16[4,128,1280]{2,1,0:T(8,128)(2,1)}), bf16[4,128,1280]{2,1,0:T(8,128)(2,1)S(1)}, u32[]{:S(2)}, u32[]{:S(2)}) async-start(bf16[4,128,1280]{2,1,0:T(8,128)(2,1)} %bitcast.279), calls=%async_computation.8 | async-start | bytes 2621440 | tf_op jit(solution)/shard_map/all_to_all | solution.py:108
  321.3 26.6 %all-to-all-done.8 = bf16[4,128,1280]{2,1,0:T(8,128)(2,1)S(1)} async-done(((bf16[4,128,1280]{2,1,0:T(8,128)(2,1)}), bf16[4,128,1280]{2,1,0:T(8,128)(2,1)S(1)}, u32[]{:S(2)}, u32[]{:S(2)}) %all-to-all-start.8) | async-done | bytes 1310752 | tf_op jit(solution)/shard_map/all_to_all | solution.py:108
  354.8 4.7 %convolution_convert_fusion = bf16[128,8192]{1,0:T(8,128)(2,1)S(1)} fusion(bf16[2,512,8192]{2,1,0:T(8,128)(2,1)} %all-gather.14.cloned.1.call-done, f32[128,512]{1,0:T(8,128)S(1)} %get-tuple-element.8, f32[512]{0:T(512)S(1)} %bitcast.325, f32[128]{0:T(128)S(1)} %add_rsqrt_fusion), kind=kOutput, calls=%fused_computation.3 | convolution fusion | flops 1074987008 | bytes 10750464 | tf_op jit(solution)/shard_map/dot_general | solution.py:137
  359.5 28.4 %all_to_all.66 = bf16[4,32,8192]{2,1,0:T(8,128)(2,1)S(1)} all-to-all(bf16[4,32,8192]{2,1,0:T(8,128)(2,1)S(1)} %bitcast.278), channel_id=1, replica_groups=mesh['dp'=4,'section'=2,'tensor'=4] {'tensor'}, dimensions={0} | all-to-all | bytes 4194304 | tf_op jit(solution)/shard_map/all_to_all | solution.py:138
  388.5 17.5 %all_to_all.67 = bf16[8,32,2048]{2,1,0:T(8,128)(2,1)S(1)} all-to-all(bf16[8,32,2048]{2,1,0:T(8,128)(2,1)S(1)} %pad_maximum_fusion), channel_id=1, replica_groups=mesh['dp'=4,'section'=2,'tensor'=4] {'section','tensor'}, dimensions={0} | all-to-all | bytes 2097152 | tf_op jit(solution)/shard_map/all_to_all | solution.py:145
  (283 shorter events, 90.2 us)
Async XLA Ops:
  10.9 11.8 %all-to-all-start = ((s32[4,1,128]{2,1,0:T(1,128)}), s32[4,1,128]{2,1,0:T(1,128)S(1)}, u32[]{:S(2)}, u32[]{:S(2)}) async-start(s32[4,1,128]{2,1,0:T(1,128)} %bitcast.3), calls=%async_computation | async-start | bytes 4096 | tf_op jit(solution)/shard_map/all_to_all | solution.py:81
  19.9 38.2 %copy-start.8 = (f32[1,8192]{1,0:T(1,128)S(1)}, f32[1,8192]{1,0:T(1,128)}, u32[]{:S(2)}) copy-start(f32[1,8192]{1,0:T(1,128)} %param.14) | copy-start | bytes 98308
  22.7 28.2 %all-to-all-start.1 = ((bf16[4,128,1024]{2,1,0:T(8,128)(2,1)}), bf16[4,128,1024]{2,1,0:T(8,128)(2,1)S(1)}, u32[]{:S(2)}, u32[]{:S(2)}) async-start(bf16[4,128,1024]{2,1,0:T(8,128)(2,1)} %bitcast.6), calls=%async_computation.1 | async-start | bytes 2097152 | tf_op jit(solution)/shard_map/all_to_all | solution.py:78
  54.4 12.9 %all-to-all-start.2 = ((bf16[8,32,1024]{2,1,0:T(8,128)(2,1)}), bf16[8,32,1024]{2,1,0:T(8,128)(2,1)S(1)}, u32[]{:S(2)}, u32[]{:S(2)}) async-start(bf16[8,32,1024]{2,1,0:T(8,128)(2,1)} %bitcast.8), calls=%async_computation.2 | async-start | bytes 1048576 | tf_op jit(solution)/shard_map/all_to_all | solution.py:91
  58.1 61.1 %all-gather.10.cloned.1.call-start = ((), (), s32[]{:S(2)}) async-start(), calls=%async_computation.12 | async-start | bytes 2621440 | tf_op jit(solution)/shard_map/all_gather | solution.py:104
  86.3 57.1 %all-gather.12.cloned.1.call-start = ((), (), s32[]{:S(2)}) async-start(), calls=%async_computation.13 | async-start | bytes 15728640 | tf_op jit(solution)/shard_map/all_gather | solution.py:57
  87.1 10.9 %copy-start.6 = (bf16[1,8192,8]{1,2,0:T(8,128)(2,1)S(1)}, bf16[1,8192,8]{1,2,0:T(8,128)(2,1)}, u32[]{:S(2)}) copy-start(bf16[1,8192,8]{1,2,0:T(8,128)(2,1)} %param.16) | copy-start | bytes 393220
  87.1 117.8 %all-gather.14.cloned.1.call-start = ((), (), s32[]{:S(2)}) async-start(), calls=%async_computation.14 | async-start | bytes 25165824 | tf_op jit(solution)/shard_map/all_gather | solution.py:57
  102.4 54.5 %copy-start.19 = (f32[64]{0:T(128)}, f32[64]{0:T(128)S(1)}, u32[]{:S(2)}) copy-start(f32[64]{0:T(128)S(1)} %get-tuple-element.63) | copy-start | bytes 772
  102.4 56.3 %copy-start.17 = (f32[64]{0:T(128)}, f32[64]{0:T(128)S(1)}, u32[]{:S(2)}) copy-start(f32[64]{0:T(128)S(1)} %get-tuple-element.64) | copy-start | bytes 772
  103.7 46.9 %copy-start.27 = (f32[64]{0:T(128)}, f32[64]{0:T(128)S(1)}, u32[]{:S(2)}) copy-start(f32[64]{0:T(128)S(1)} %get-tuple-element.67) | copy-start | bytes 772
  103.7 52.8 %copy-start.25 = (f32[64]{0:T(128)}, f32[64]{0:T(128)S(1)}, u32[]{:S(2)}) copy-start(f32[64]{0:T(128)S(1)} %get-tuple-element.70) | copy-start | bytes 772
  103.7 55.0 %copy-start.21 = (f32[64]{0:T(128)}, f32[64]{0:T(128)S(1)}, u32[]{:S(2)}) copy-start(f32[64]{0:T(128)S(1)} %get-tuple-element.68) | copy-start | bytes 772
  103.7 55.0 %copy-start.23 = (f32[64]{0:T(128)}, f32[64]{0:T(128)S(1)}, u32[]{:S(2)}) copy-start(f32[64]{0:T(128)S(1)} %get-tuple-element.69) | copy-start | bytes 772
  105.7 86.9 %copy-start.15 = (pred[64,64]{1,0:T(8,128)(4,1)}, pred[64,64]{1,0:T(8,128)(4,1)S(1)}, u32[]{:S(2)}) copy-start(pred[64,64]{1,0:T(8,128)(4,1)S(1)} %fusion.173) | copy-start | bytes 12292
  122.0 10.2 %all-to-all-start.5 = ((f32[4,128,8]{1,2,0:T(8,128)}), f32[4,128,8]{1,2,0:T(8,128)S(1)}, u32[]{:S(2)}, u32[]{:S(2)}) async-start(f32[4,128,8]{1,2,0:T(8,128)} %fusion.166), calls=%async_computation.5 | async-start | bytes 32768 | tf_op jit(solution)/shard_map/all_to_all | solution.py:109
  126.6 28.8 %copy-start.30 = (f32[64]{0:T(128)}, f32[64]{0:T(128)S(1)}, u32[]{:S(2)}) copy-start(f32[64]{0:T(128)S(1)} %compare_convert_fusion.2) | copy-start | bytes 772
  150.5 36.8 %all-to-all-start.4 = ((bf16[4,128,1280]{2,1,0:T(8,128)(2,1)}), bf16[4,128,1280]{2,1,0:T(8,128)(2,1)}, u32[]{:S(2)}, u32[]{:S(2)}) async-start(bf16[4,128,1280]{2,1,0:T(8,128)(2,1)} %bitcast.280), calls=%async_computation.4 | async-start | bytes 2621440 | tf_op jit(solution)/shard_map/all_to_all | solution.py:108
  211.0 30.1 %all-to-all-start.6 = ((bf16[4,32,8192]{2,1,0:T(8,128)(2,1)}), bf16[4,32,8192]{2,1,0:T(8,128)(2,1)}, u32[]{:S(2)}, u32[]{:S(2)}) async-start(bf16[4,32,8192]{2,1,0:T(8,128)(2,1)} %bitcast.277), calls=%async_computation.6 | async-start | bytes 4194304 | tf_op jit(solution)/shard_map/all_to_all | solution.py:138
  215.7 82.4 %all-gather.16.cloned.1.call-start = ((), (), s32[]{:S(2)}) async-start(), calls=%async_computation.15 | async-start | bytes 2621440 | tf_op jit(solution)/shard_map/all_gather | solution.py:104
  301.0 11.1 %all-to-all-start.9 = ((f32[4,128,8]{1,2,0:T(8,128)}), f32[4,128,8]{1,2,0:T(8,128)S(1)}, u32[]{:S(2)}, u32[]{:S(2)}) async-start(f32[4,128,8]{1,2,0:T(8,128)} %fusion.164), calls=%async_computation.9 | async-start | bytes 32768 | tf_op jit(solution)/shard_map/all_to_all | solution.py:109
  312.1 35.7 %all-to-all-start.8 = ((bf16[4,128,1280]{2,1,0:T(8,128)(2,1)}), bf16[4,128,1280]{2,1,0:T(8,128)(2,1)S(1)}, u32[]{:S(2)}, u32[]{:S(2)}) async-start(bf16[4,128,1280]{2,1,0:T(8,128)(2,1)} %bitcast.279), calls=%async_computation.8 | async-start | bytes 2621440 | tf_op jit(solution)/shard_map/all_to_all | solution.py:108
  321.2 30.4 %copy-start.16 = (pred[64,64]{1,0:T(8,128)(4,1)S(1)}, pred[64,64]{1,0:T(8,128)(4,1)}, u32[]{:S(2)}) copy-start(pred[64,64]{1,0:T(8,128)(4,1)} %copy-done.15) | copy-start | bytes 12292
  388.4 18.6 %copy-start.1 = (bf16[256,2048]{1,0:T(8,128)(2,1)S(1)}, bf16[256,2048]{1,0:T(8,128)(2,1)}, u32[]{:S(2)}) copy-start(bf16[256,2048]{1,0:T(8,128)(2,1)} %param.11) | copy-start | bytes 3145732
  (28 other events, 150.3 us)
Sparse Core Ops, SparseCore 0:
  86.4 32.6 all-gather.9
  120.7 22.6 all-gather.11
  144.9 31.2 all-gather.13
  264.7 33.2 all-gather.15
where the time goes:
time: 415 us; the launch traced here: 414 us
  waiting for transfers between devices  172 us (41%)
  blocking collectives  101 us (24%)
  matrix products  42.6 us (10%)
  starting transfers between devices  37.5 us (9%)
  local copies, waits for them, and re-layouts  25.3 us (6%)
  other arithmetic  19.1 us (5%)
  between operations  15.9 us (4%)
    all_to_all x2, waiting for transfers between devices, per_device(): lax.all_to_all(proj.reshape(groups, half, -1), 'dp', 0, 0, tiled=True)  54.5 us
    all_gather x2, waiting for transfers between devices, per_device(): full_u = lax.all_gather(u, 'tensor', axis=1, tiled=True)  45.6 us
    all_to_all x2, blocking collectives, per_device(): u = lax.all_to_all(u, 'dp', 0, 0, tiled=True)  35.7 us
    all_to_all x1, blocking collectives, per_device(): lax.all_to_all(partial_value.reshape(width, few, feats), 'tensor', 0, 0,...  28.4 us
    all_to_all x1, waiting for transfers between devices, per_device(): lax.all_to_all(partial_value.reshape(width, few, feats), 'tensor', 0, 0,...  25.4 us
    all_to_all x1, waiting for transfers between devices, per_device(): lax.all_to_all(outbox.reshape(groups, capacity, part), 'dp', split_axis=0...  24.7 us
    all_to_all x1, blocking collectives, per_device(): outs = lax.all_to_all(outs, ('section', 'tensor'), 0, 0, tiled=True)  17.5 us
    dot_general x2, matrix products, per_device(): proj = jnp.dot(full_u, w_in[layer], preferred_element_type=f32).astype(bf16)  13.6 us
  transfers between devices with their start and end apart: 12, of which 10 were waited for; matrix products, arithmetic and copies ran while one was open for 13% of the time, Pallas kernels for 0%

commit v1 on v0

--- a/solution.py
+++ b/solution.py
@@ -101,7 +101,16 @@
         u = u.reshape(few, groups, depth).transpose(1, 0, 2)
         u = lax.all_to_all(u, "dp", 0, 0, tiled=True)
         step_w = lax.dynamic_slice_in_dim(w_step[layer], dp_idx * depth, depth, axis=0)
-        full_u = lax.all_gather(u, "tensor", axis=1, tiled=True)
+        ring = [u]
+        for hop in range(3):
+            ring.append(
+                lax.ppermute(ring[-1], "tensor", [(dev, (dev + 1) % 4) for dev in range(4)])
+            )
+        full_u = jnp.roll(
+            jnp.concatenate(ring[::-1], axis=1),
+            (lax.axis_index("tensor") + 1) * ring[0].shape[1],
+            axis=1,
+        )
         full_u = full_u.reshape(groups * half, depth)
         proj = jnp.dot(full_u, w_in[layer], preferred_element_type=f32).astype(bf16)
         pre = jnp.dot(full_u, step_w, preferred_element_type=f32)

time: 415 us -> 423 us (1.019)
  blocking collectives: 101 us -> 83.5 us
  waiting for transfers between devices: 172 us -> 189 us
  other arithmetic: 19.1 us -> 28 us
  matrix products: 42.6 us -> 38.2 us
    ppermute x0 -> x6, waiting for transfers between devices: none -> 64.7 us  [per_device(): lax.ppermute(ring[-1], 'tensor', [(dev, (dev + 1) % 4) for dev in range(4)])]
    all_gather x2 -> x0, waiting for transfers between devices: 45.6 us -> none  [per_device(): full_u = lax.all_gather(u, 'tensor', axis=1, tiled=True)]
    all_to_all x2 -> x1, blocking collectives: 35.7 us -> 17.4 us  [per_device(): u = lax.all_to_all(u, 'dp', 0, 0, tiled=True)]
    all_to_all x0 -> x1, waiting for transfers between devices: none -> 10.4 us  [per_device(): u = lax.all_to_all(u, 'dp', 0, 0, tiled=True)]
    concatenate x0 -> x2, other arithmetic: none -> 9.87 us  [per_device(): jnp.roll(jnp.concatenate(ring[::-1], axis=1), (lax.axis_index('tensor') +...]
    all_gather x2, waiting for transfers between devices: 7.31 us -> 0.02 us  [whole(): return lax.all_gather(param, 'section', axis=0, tiled=True)]
  transfers between devices with their start and end apart: 12 -> 17, of which waited for: 10 -> 14; matrix products, arithmetic and copies ran while one was open for 13% -> 15% of each run, Pallas kernels for 0% -> 0%
where the time goes in v1:
time: 423 us; the launch traced here: 422 us
  waiting for transfers between devices  189 us (45%)
  blocking collectives  83.5 us (20%)
  starting transfers between devices  40.1 us (9%)
  matrix products  38.2 us (9%)
  other arithmetic  28 us (7%)
  local copies, waits for them, and re-layouts  26.2 us (6%)
  between operations  16.3 us (4%)
    ppermute x6, waiting for transfers between devices, per_device(): lax.ppermute(ring[-1], 'tensor', [(dev, (dev + 1) % 4) for dev in range(4)])  64.7 us
    all_to_all x2, waiting for transfers between devices, per_device(): lax.all_to_all(proj.reshape(groups, half, -1), 'dp', 0, 0, tiled=True)  51.4 us
    all_to_all x1, blocking collectives, per_device(): lax.all_to_all(partial_value.reshape(width, few, feats), 'tensor', 0, 0,...  28.6 us
    all_to_all x1, waiting for transfers between devices, per_device(): lax.all_to_all(partial_value.reshape(width, few, feats), 'tensor', 0, 0,...  26.2 us
    all_to_all x1, waiting for transfers between devices, per_device(): lax.all_to_all(outbox.reshape(groups, capacity, part), 'dp', split_axis=0...  24.4 us
    all_to_all x1, blocking collectives, per_device(): outs = lax.all_to_all(outs, ('section', 'tensor'), 0, 0, tiled=True)  17.5 us
    all_to_all x1, blocking collectives, per_device(): u = lax.all_to_all(u, 'dp', 0, 0, tiled=True)  17.4 us
    dot_general x2, matrix products, per_device(): proj = jnp.dot(full_u, w_in[layer], preferred_element_type=f32).astype(bf16)  13.6 us
  transfers between devices with their start and end apart: 17, of which 14 were waited for; matrix products, arithmetic and copies ran while one was open for 15% of the time, Pallas kernels for 0%

profile of v1, /device:TPU:0, one launch (start us, length us, event | category | flops | bytes accessed | tf_op | source)
XLA Modules:
  0.0 421.5 jit_solution(2271183598660476261)
XLA Ops:
  11.6 6.3 %all-to-all-start = ((s32[4,1,128]{2,1,0:T(1,128)}), s32[4,1,128]{2,1,0:T(1,128)S(1)}, u32[]{:S(2)}, u32[]{:S(2)}) async-start(s32[4,1,128]{2,1,0:T(1,128)} %bitcast.3), calls=%async_computation | async-start | bytes 4096 | tf_op jit(solution)/shard_map/all_to_all | solution.py:81
  27.1 24.4 %all-to-all-done.1 = bf16[4,128,1024]{2,1,0:T(8,128)(2,1)S(1)} async-done(((bf16[4,128,1024]{2,1,0:T(8,128)(2,1)}), bf16[4,128,1024]{2,1,0:T(8,128)(2,1)S(1)}, u32[]{:S(2)}, u32[]{:S(2)}) %all-to-all-start.1) | async-done | bytes 1048608 | tf_op jit(solution)/shard_map/all_to_all | solution.py:78
  63.8 4.0 all-to-all-done.2
  77.6 10.4 %all-to-all-done.3 = bf16[4,32,2048]{2,1,0:T(8,128)(2,1)S(1)} async-done(((bf16[4,32,2048]{2,1,0:T(8,128)(2,1)}), bf16[4,32,2048]{2,1,0:T(8,128)(2,1)S(1)}, u32[]{:S(2)}, u32[]{:S(2)}) %all-to-all-start.3) | async-done | bytes 524320 | tf_op jit(solution)/shard_map/all_to_all | solution.py:102
  95.8 6.5 %collective-permute-done = bf16[4,32,2048]{2,1,0:T(8,128)(2,1)S(1)} collective-permute-done((bf16[4,32,2048]{2,1,0:T(8,128)(2,1)S(1)}, bf16[4,32,2048]{2,1,0:T(8,128)(2,1)S(1)}, u32[]{:S(2)}, u32[]{:S(2)}) %collective-permute-start) | collective-permute-done | bytes 524320 | tf_op jit(solution)/shard_map/ppermute | solution.py:107
  104.9 10.8 %collective-permute-done.1 = bf16[4,32,2048]{2,1,0:T(8,128)(2,1)S(1)} collective-permute-done((bf16[4,32,2048]{2,1,0:T(8,128)(2,1)S(1)}, bf16[4,32,2048]{2,1,0:T(8,128)(2,1)S(1)}, u32[]{:S(2)}, u32[]{:S(2)}) %collective-permute-start.1) | collective-permute-done | bytes 524320 | tf_op jit(solution)/shard_map/ppermute | solution.py:107
  117.9 10.4 %collective-permute-done.2 = bf16[4,32,2048]{2,1,0:T(8,128)(2,1)} collective-permute-done((bf16[4,32,2048]{2,1,0:T(8,128)(2,1)S(1)}, bf16[4,32,2048]{2,1,0:T(8,128)(2,1)}, u32[]{:S(2)}, u32[]{:S(2)}) %collective-permute-start.2) | collective-permute-done | bytes 524320 | tf_op jit(solution)/shard_map/ppermute | solution.py:107
  128.4 5.2 %fusion.14 = bf16[4,128,2048]{2,1,0:T(8,128)(2,1)S(1)} fusion(s32[]{:T(128)S(6)} %select_n.132, bf16[4,32,2048]{2,1,0:T(8,128)(2,1)} %collective-permute-done.2, bf16[4,32,2048]{2,1,0:T(8,128)(2,1)S(1)} %collective-permute-done.1, bf16[4,32,2048]{2,1,0:T(8,128)(2,1)S(1)} %collective-permute-done, bf16[4,32,2048]{2,1,0:T(8,128)(2,1)S(1)} %all-to-all-done.3), kind=kLoop, calls=%fused_computation.41 | loop fusion | flops 16777216 | bytes 4194308 | tf_op jit(solution)/shard_map/jit(_roll_dynamic)/concatenate | solution.py:109
  148.2 7.2 %fusion.2 = bf16[512,1280]{1,0:T(8,128)(2,1)} fusion(bf16[512,2048]{1,0:T(8,128)(2,1)} %bitcast.269, bf16[2,2048,1280]{2,1,0:T(8,128)(2,1)} %all-gather.8.cloned.1.call-done), kind=kOutput, calls=%fused_computation.29 | convolution fusion | flops 2685009920 | bytes 8650752 | tf_op jit(solution)/shard_map/dot_general | solution.py:115
  163.3 27.5 %all-to-all-done.4 = bf16[4,128,1280]{2,1,0:T(8,128)(2,1)S(1)} async-done(((bf16[4,128,1280]{2,1,0:T(8,128)(2,1)}), bf16[4,128,1280]{2,1,0:T(8,128)(2,1)S(1)}, u32[]{:S(2)}, u32[]{:S(2)}) %all-to-all-start.4) | async-done | bytes 1310752 | tf_op jit(solution)/shard_map/all_to_all | solution.py:117
  205.6 6.0 %convolution_convert_fusion.1 = bf16[128,8192]{1,0:T(8,128)(2,1)} fusion(bf16[2,512,8192]{2,1,0:T(8,128)(2,1)} %all-gather.10.cloned.1.call-done, f32[128,512]{1,0:T(8,128)S(1)} %get-tuple-element.15, f32[512]{0:T(512)} %bitcast.323, f32[128]{0:T(128)S(1)} %add_rsqrt_fusion.2), kind=kOutput, calls=%fused_computation.4 | convolution fusion | flops 1074987008 | bytes 10750464 | tf_op jit(solution)/shard_map/dot_general | solution.py:146
  211.6 4.6 %all-to-all-start.6 = ((bf16[4,32,8192]{2,1,0:T(8,128)(2,1)}), bf16[4,32,8192]{2,1,0:T(8,128)(2,1)}, u32[]{:S(2)}, u32[]{:S(2)}) async-start(bf16[4,32,8192]{2,1,0:T(8,128)(2,1)} %bitcast.274), calls=%async_computation.6 | async-start | bytes 4194304 | tf_op jit(solution)/shard_map/all_to_all | solution.py:147
  216.2 26.2 %all-to-all-done.6 = bf16[4,32,8192]{2,1,0:T(8,128)(2,1)} async-done(((bf16[4,32,8192]{2,1,0:T(8,128)(2,1)}), bf16[4,32,8192]{2,1,0:T(8,128)(2,1)}, u32[]{:S(2)}, u32[]{:S(2)}) %all-to-all-start.6) | async-done | bytes 2097184 | tf_op jit(solution)/shard_map/all_to_all | solution.py:147
  249.3 17.4 %all_to_all.64 = bf16[4,32,2048]{2,1,0:T(8,128)(2,1)S(1)} all-to-all(bf16[4,32,2048]{2,1,0:T(8,128)(2,1)S(1)} %get-tuple-element.12), channel_id=1, replica_groups=mesh['dp'=4,'section'=2,'tensor'=4] {'dp'}, dimensions={0} | all-to-all | bytes 1048576 | tf_op jit(solution)/shard_map/all_to_all | solution.py:102
  268.1 12.4 %collective-permute-done.3 = bf16[4,32,2048]{2,1,0:T(8,128)(2,1)S(1)} collective-permute-done((bf16[4,32,2048]{2,1,0:T(8,128)(2,1)S(1)}, bf16[4,32,2048]{2,1,0:T(8,128)(2,1)S(1)}, u32[]{:S(2)}, u32[]{:S(2)}) %collective-permute-start.3) | collective-permute-done | bytes 524320 | tf_op jit(solution)/shard_map/ppermute | solution.py:107
  281.1 12.5 %collective-permute-done.4 = bf16[4,32,2048]{2,1,0:T(8,128)(2,1)S(1)} collective-permute-done((bf16[4,32,2048]{2,1,0:T(8,128)(2,1)S(1)}, bf16[4,32,2048]{2,1,0:T(8,128)(2,1)S(1)}, u32[]{:S(2)}, u32[]{:S(2)}) %collective-permute-start.4) | collective-permute-done | bytes 524320 | tf_op jit(solution)/shard_map/ppermute | solution.py:107
  293.6 12.1 %collective-permute-done.5 = bf16[4,32,2048]{2,1,0:T(8,128)(2,1)S(1)} collective-permute-done((bf16[4,32,2048]{2,1,0:T(8,128)(2,1)S(1)}, bf16[4,32,2048]{2,1,0:T(8,128)(2,1)S(1)}, u32[]{:S(2)}, u32[]{:S(2)}) %collective-permute-start.5) | collective-permute-done | bytes 524320 | tf_op jit(solution)/shard_map/ppermute | solution.py:107
  305.7 4.6 %fusion.7 = bf16[4,128,2048]{2,1,0:T(8,128)(2,1)S(1)} fusion(s32[]{:T(128)S(6)} %select_n.132, bf16[4,32,2048]{2,1,0:T(8,128)(2,1)S(1)} %collective-permute-done.5, bf16[4,32,2048]{2,1,0:T(8,128)(2,1)S(1)} %collective-permute-done.4, bf16[4,32,2048]{2,1,0:T(8,128)(2,1)S(1)} %collective-permute-done.3, bf16[4,32,2048]{2,1,0:T(8,128)(2,1)S(1)} %all_to_all.64), kind=kLoop, calls=%fused_computation.34 | loop fusion | flops 16777216 | bytes 4194308 | tf_op jit(solution)/shard_map/jit(_roll_dynamic)/concatenate | solution.py:109
  316.1 6.4 %fusion.3 = bf16[512,1280]{1,0:T(8,128)(2,1)} fusion(bf16[512,2048]{1,0:T(8,128)(2,1)S(1)} %bitcast.270, bf16[2,2048,1280]{2,1,0:T(8,128)(2,1)} %all-gather.8.cloned.1.call-done), kind=kOutput, calls=%fused_computation.30 | convolution fusion | flops 2685009920 | bytes 8650752 | tf_op jit(solution)/shard_map/dot_general | solution.py:115
  322.6 5.2 %all-to-all-start.8 = ((bf16[4,128,1280]{2,1,0:T(8,128)(2,1)}), bf16[4,128,1280]{2,1,0:T(8,128)(2,1)S(1)}, u32[]{:S(2)}, u32[]{:S(2)}) async-start(bf16[4,128,1280]{2,1,0:T(8,128)(2,1)} %bitcast.276), calls=%async_computation.8 | async-start | bytes 2621440 | tf_op jit(solution)/shard_map/all_to_all | solution.py:117
  331.8 23.8 %all-to-all-done.8 = bf16[4,128,1280]{2,1,0:T(8,128)(2,1)S(1)} async-done(((bf16[4,128,1280]{2,1,0:T(8,128)(2,1)}), bf16[4,128,1280]{2,1,0:T(8,128)(2,1)S(1)}, u32[]{:S(2)}, u32[]{:S(2)}) %all-to-all-start.8) | async-done | bytes 1310752 | tf_op jit(solution)/shard_map/all_to_all | solution.py:117
  362.4 4.7 %convolution_convert_fusion = bf16[128,8192]{1,0:T(8,128)(2,1)S(1)} fusion(bf16[2,512,8192]{2,1,0:T(8,128)(2,1)} %all-gather.10.cloned.1.call-done, f32[128,512]{1,0:T(8,128)S(1)} %get-tuple-element.9, f32[512]{0:T(512)S(1)} %bitcast.322, f32[128]{0:T(128)S(1)} %add_rsqrt_fusion), kind=kOutput, calls=%fused_computation.3 | convolution fusion | flops 1074987008 | bytes 10750464 | tf_op jit(solution)/shard_map/dot_general | solution.py:146
  367.1 28.6 %all_to_all.65 = bf16[4,32,8192]{2,1,0:T(8,128)(2,1)S(1)} all-to-all(bf16[4,32,8192]{2,1,0:T(8,128)(2,1)S(1)} %bitcast.275), channel_id=1, replica_groups=mesh['dp'=4,'section'=2,'tensor'=4] {'tensor'}, dimensions={0} | all-to-all | bytes 4194304 | tf_op jit(solution)/shard_map/all_to_all | solution.py:147
  396.2 17.5 %all_to_all.66 = bf16[8,32,2048]{2,1,0:T(8,128)(2,1)S(1)} all-to-all(bf16[8,32,2048]{2,1,0:T(8,128)(2,1)S(1)} %pad_maximum_fusion), channel_id=1, replica_groups=mesh['dp'=4,'section'=2,'tensor'=4] {'section','tensor'}, dimensions={0} | all-to-all | bytes 2097152 | tf_op jit(solution)/shard_map/all_to_all | solution.py:154
  (292 shorter events, 110.2 us)
Async XLA Ops:
  6.5 141.6 %all-gather.8.cloned.1.call-start = ((), (), s32[]{:S(2)}) async-start(), calls=%async_computation.12 | async-start | bytes 15728640 | tf_op jit(solution)/shard_map/all_gather | solution.py:57
  7.3 198.3 %all-gather.10.cloned.1.call-start = ((), (), s32[]{:S(2)}) async-start(), calls=%async_computation.13 | async-start | bytes 25165824 | tf_op jit(solution)/shard_map/all_gather | solution.py:57
  11.6 11.9 %all-to-all-start = ((s32[4,1,128]{2,1,0:T(1,128)}), s32[4,1,128]{2,1,0:T(1,128)S(1)}, u32[]{:S(2)}, u32[]{:S(2)}) async-start(s32[4,1,128]{2,1,0:T(1,128)} %bitcast.3), calls=%async_computation | async-start | bytes 4096 | tf_op jit(solution)/shard_map/all_to_all | solution.py:81
  23.6 28.0 %all-to-all-start.1 = ((bf16[4,128,1024]{2,1,0:T(8,128)(2,1)}), bf16[4,128,1024]{2,1,0:T(8,128)(2,1)S(1)}, u32[]{:S(2)}, u32[]{:S(2)}) async-start(bf16[4,128,1024]{2,1,0:T(8,128)(2,1)} %bitcast.6), calls=%async_computation.1 | async-start | bytes 2097152 | tf_op jit(solution)/shard_map/all_to_all | solution.py:78
  55.0 12.9 %all-to-all-start.2 = ((bf16[8,32,1024]{2,1,0:T(8,128)(2,1)}), bf16[8,32,1024]{2,1,0:T(8,128)(2,1)S(1)}, u32[]{:S(2)}, u32[]{:S(2)}) async-start(bf16[8,32,1024]{2,1,0:T(8,128)(2,1)} %bitcast.8), calls=%async_computation.2 | async-start | bytes 1048576 | tf_op jit(solution)/shard_map/all_to_all | solution.py:91
  69.2 18.8 %all-to-all-start.3 = ((bf16[4,32,2048]{2,1,0:T(8,128)(2,1)}), bf16[4,32,2048]{2,1,0:T(8,128)(2,1)S(1)}, u32[]{:S(2)}, u32[]{:S(2)}) async-start(bf16[4,32,2048]{2,1,0:T(8,128)(2,1)} %fusion.42), calls=%async_computation.3 | async-start | bytes 1048576 | tf_op jit(solution)/shard_map/all_to_all | solution.py:102
  88.0 14.3 %collective-permute-start = (bf16[4,32,2048]{2,1,0:T(8,128)(2,1)S(1)}, bf16[4,32,2048]{2,1,0:T(8,128)(2,1)S(1)}, u32[]{:S(2)}, u32[]{:S(2)}) collective-permute-start(bf16[4,32,2048]{2,1,0:T(8,128)(2,1)S(1)} %all-to-all-done.3), channel_id=1, source_target_pairs={{0,1},{1,2},{2,3},{3,0},{4,5},{5,6},{6,7},{7,4},{8,9},{9,10},{10,1... | collective-permute-start | bytes 1572872 | tf_op jit(solution)/shard_map/ppermute | solution.py:107
  95.2 63.7 %copy-start.25 = (f32[64]{0:T(128)}, f32[64]{0:T(128)S(1)}, u32[]{:S(2)}) copy-start(f32[64]{0:T(128)S(1)} %get-tuple-element.71) | copy-start | bytes 772
  95.2 64.5 %copy-start.23 = (f32[64]{0:T(128)}, f32[64]{0:T(128)S(1)}, u32[]{:S(2)}) copy-start(f32[64]{0:T(128)S(1)} %get-tuple-element.68) | copy-start | bytes 772
  95.2 67.4 %copy-start.19 = (f32[64]{0:T(128)}, f32[64]{0:T(128)S(1)}, u32[]{:S(2)}) copy-start(f32[64]{0:T(128)S(1)} %get-tuple-element.69) | copy-start | bytes 772
  95.2 67.3 %copy-start.21 = (f32[64]{0:T(128)}, f32[64]{0:T(128)S(1)}, u32[]{:S(2)}) copy-start(f32[64]{0:T(128)S(1)} %get-tuple-element.70) | copy-start | bytes 772
  102.3 13.4 %collective-permute-start.1 = (bf16[4,32,2048]{2,1,0:T(8,128)(2,1)S(1)}, bf16[4,32,2048]{2,1,0:T(8,128)(2,1)S(1)}, u32[]{:S(2)}, u32[]{:S(2)}) collective-permute-start(bf16[4,32,2048]{2,1,0:T(8,128)(2,1)S(1)} %collective-permute-done), channel_id=1, source_target_pairs={{0,1},{1,2},{2,3},{3,0},{4,5},{5,6},{6,7},{7,4},{8,9},{9,10},{10,1... | collective-permute-start | bytes 1572872 | tf_op jit(solution)/shard_map/ppermute | solution.py:107
  104.9 89.4 %copy-start.11 = (pred[64,64]{1,0:T(8,128)(4,1)}, pred[64,64]{1,0:T(8,128)(4,1)S(1)}, u32[]{:S(2)}) copy-start(pred[64,64]{1,0:T(8,128)(4,1)S(1)} %fusion.187) | copy-start | bytes 12292
  104.9 91.0 %copy-start.9 = (pred[64,64]{1,0:T(8,128)(4,1)}, pred[64,64]{1,0:T(8,128)(4,1)S(1)}, u32[]{:S(2)}) copy-start(pred[64,64]{1,0:T(8,128)(4,1)S(1)} %fusion.186) | copy-start | bytes 12292
  115.7 12.7 %collective-permute-start.2 = (bf16[4,32,2048]{2,1,0:T(8,128)(2,1)S(1)}, bf16[4,32,2048]{2,1,0:T(8,128)(2,1)}, u32[]{:S(2)}, u32[]{:S(2)}) collective-permute-start(bf16[4,32,2048]{2,1,0:T(8,128)(2,1)S(1)} %collective-permute-done.1), channel_id=1, source_target_pairs={{0,1},{1,2},{2,3},{3,0},{4,5},{5,6},{6,7},{7,4},{8,9},{9,10},{10,1... | collective-permute-start | bytes 1572872 | tf_op jit(solution)/shard_map/ppermute | solution.py:107
  116.3 80.0 %copy-start.8 = (f32[8]{0:T(128)}, f32[8]{0:T(128)S(1)}, u32[]{:S(2)}) copy-start(f32[8]{0:T(128)S(1)} %get-tuple-element.53) | copy-start | bytes 100
  136.2 8.8 %all-to-all-start.5 = ((f32[4,128,8]{1,2,0:T(8,128)}), f32[4,128,8]{1,2,0:T(8,128)S(1)}, u32[]{:S(2)}, u32[]{:S(2)}) async-start(f32[4,128,8]{1,2,0:T(8,128)} %fusion.180), calls=%async_computation.5 | async-start | bytes 32768 | tf_op jit(solution)/shard_map/all_to_all | solution.py:118
  155.3 35.5 %all-to-all-start.4 = ((bf16[4,128,1280]{2,1,0:T(8,128)(2,1)}), bf16[4,128,1280]{2,1,0:T(8,128)(2,1)S(1)}, u32[]{:S(2)}, u32[]{:S(2)}) async-start(bf16[4,128,1280]{2,1,0:T(8,128)(2,1)} %bitcast.277), calls=%async_computation.4 | async-start | bytes 2621440 | tf_op jit(solution)/shard_map/all_to_all | solution.py:117
  211.6 30.9 %all-to-all-start.6 = ((bf16[4,32,8192]{2,1,0:T(8,128)(2,1)}), bf16[4,32,8192]{2,1,0:T(8,128)(2,1)}, u32[]{:S(2)}, u32[]{:S(2)}) async-start(bf16[4,32,8192]{2,1,0:T(8,128)(2,1)} %bitcast.274), calls=%async_computation.6 | async-start | bytes 4194304 | tf_op jit(solution)/shard_map/all_to_all | solution.py:147
  266.7 13.9 %collective-permute-start.3 = (bf16[4,32,2048]{2,1,0:T(8,128)(2,1)S(1)}, bf16[4,32,2048]{2,1,0:T(8,128)(2,1)S(1)}, u32[]{:S(2)}, u32[]{:S(2)}) collective-permute-start(bf16[4,32,2048]{2,1,0:T(8,128)(2,1)S(1)} %all_to_all.64), channel_id=1, source_target_pairs={{0,1},{1,2},{2,3},{3,0},{4,5},{5,6},{6,7},{7,4},{8,9},{9,10},{10,1... | collective-permute-start | bytes 1572872 | tf_op jit(solution)/shard_map/ppermute | solution.py:107
  280.6 13.0 %collective-permute-start.4 = (bf16[4,32,2048]{2,1,0:T(8,128)(2,1)S(1)}, bf16[4,32,2048]{2,1,0:T(8,128)(2,1)S(1)}, u32[]{:S(2)}, u32[]{:S(2)}) collective-permute-start(bf16[4,32,2048]{2,1,0:T(8,128)(2,1)S(1)} %collective-permute-done.3), channel_id=1, source_target_pairs={{0,1},{1,2},{2,3},{3,0},{4,5},{5,6},{6,7},{7,4},{8,9},{9,10},{10,1... | collective-permute-start | bytes 1572872 | tf_op jit(solution)/shard_map/ppermute | solution.py:107
  293.6 12.2 %collective-permute-start.5 = (bf16[4,32,2048]{2,1,0:T(8,128)(2,1)S(1)}, bf16[4,32,2048]{2,1,0:T(8,128)(2,1)S(1)}, u32[]{:S(2)}, u32[]{:S(2)}) collective-permute-start(bf16[4,32,2048]{2,1,0:T(8,128)(2,1)S(1)} %collective-permute-done.4), channel_id=1, source_target_pairs={{0,1},{1,2},{2,3},{3,0},{4,5},{5,6},{6,7},{7,4},{8,9},{9,10},{10,1... | collective-permute-start | bytes 1572872 | tf_op jit(solution)/shard_map/ppermute | solution.py:107
  312.4 10.2 %all-to-all-start.9 = ((f32[4,128,8]{1,2,0:T(8,128)}), f32[4,128,8]{1,2,0:T(8,128)S(1)}, u32[]{:S(2)}, u32[]{:S(2)}) async-start(f32[4,128,8]{1,2,0:T(8,128)} %fusion.178), calls=%async_computation.9 | async-start | bytes 32768 | tf_op jit(solution)/shard_map/all_to_all | solution.py:118
  322.6 33.0 %all-to-all-start.8 = ((bf16[4,128,1280]{2,1,0:T(8,128)(2,1)}), bf16[4,128,1280]{2,1,0:T(8,128)(2,1)S(1)}, u32[]{:S(2)}, u32[]{:S(2)}) async-start(bf16[4,128,1280]{2,1,0:T(8,128)(2,1)} %bitcast.276), calls=%async_computation.8 | async-start | bytes 2621440 | tf_op jit(solution)/shard_map/all_to_all | solution.py:117
  (33 other events, 739.8 us)
Sparse Core Ops, SparseCore 0:
  8.9 25.3 all-gather.7
  35.8 31.5 all-gather.9
